TPU v7x, 32 devices: a whole 2x2x4 slice. The times are simulated.
32 devices in a mesh: groups: 2 (over y), req: 2 (over x), head: 4 (over z), sec: 2 (over core).
Axes of the slice: x: 2, y: 2, z: 4, core: 2. Of those that a mesh axis runs over, the one named last changes fastest.
Arguments:
- queries: bfloat16 [512, 4096], P(('groups', 'req'), ('head', 'sec')), parts along dimension 0, may hold values from -16 to 16
- cache_pool: bfloat16 [48, 128, 8, 128], P(('groups', 'req'), None, 'head'), parts along dimension 0, may hold values from -4 to 4
- lengths: int32 [4], P(('groups', 'req')), parts along dimension 0, may hold values from 128 to 1536, as said below
- block_table: int32 [4, 12], P(('groups', 'req')), parts along dimension 0, may hold values from 0 to 11, as said below
- out_proj: bfloat16 [4096, 2880], P(('head', 'sec')), may hold values from -0.375 to 0.375
- residual_in: bfloat16 [512, 2880], P(('groups', 'req', 'head', 'sec')), parts along dimension 0, may hold values from -16 to 16
- norm_gain: float32 [2880], replicated, may hold values from 0.1 to 1.9
- expert_ids: int32 [512, 4], P(('groups', 'req', 'head', 'sec')), parts along dimension 0, may hold values from 0 to 7, all different within a row; in each aligned block of 16 rows (0 to 15, 16 to 31, ...) at most 8 rows name the same one
- route_weight: float32 [512, 4], P(('groups', 'req', 'head', 'sec')), parts along dimension 0, may hold values from 0.2 to 1
- gate_weight: bfloat16 [8, 2880, 2880], P(('head', 'sec'), None, 'req'), may hold values from -0.109375 to 0.109375
- up_weight: bfloat16 [8, 2880, 2880], P(('head', 'sec'), None, 'req'), may hold values from -0.109375 to 0.109375
- down_weight: bfloat16 [8, 2880, 2880], P(('head', 'sec'), 'req'), may hold values from -0.109375 to 0.109375
Outputs:
- layer_out: bfloat16 [512, 2880], P(('groups', 'req', 'head', 'sec')), parts along dimension 0
There are 2 independent parts, one for each index of `groups`. A program takes and returns all parts, laid end to end along the dimension named above; an argument that names none is the same for every part. Nothing has to cross between parts.
Inputs may be any that keep to these rules, and one draw needn't show every extreme that they name: lengths[r] counts request r's positions, its last 128 positions being its new rows; some request reaches 1536 in every draw. `block_table`: each row is a permutation of 0 to 11. `expert_ids`: a row names 4 different experts; in each aligned block of 16 rows every expert is named by exactly 8 rows.
All inputs are finite; a program needn't handle non-finite values.
Results may differ from a plain program's by a relative error of at most 0.017.
Values may be sent and summed in bfloat16 or wider, within the bound.
A program may use at most 128 MiB of HBM per device.

v0:
```python
import math

import jax
import jax.numpy as jnp
from jax import lax
from jax.sharding import PartitionSpec as P

QH = 64
KVH = 8
TOP = 4


EPSILON = 1e-05
MASKED = -1e30


def run_expert(row_block, gate_weight, up_weight, down_weight):
    row_shape = row_block.shape
    flat_rows = row_block.reshape(-1, row_shape[-1])
    gate_out = jnp.dot(flat_rows, gate_weight[0], preferred_element_type=jnp.float32)
    up_out = jnp.dot(flat_rows, up_weight[0], preferred_element_type=jnp.float32)
    activated = (gate_out * jax.nn.sigmoid(1.702 * gate_out) * (up_out + 1.0)).astype(jnp.bfloat16)
    partial_value = jnp.dot(activated, down_weight[0], preferred_element_type=jnp.float32)
    return partial_value.astype(jnp.bfloat16).reshape(row_shape[:-1] + (partial_value.shape[-1],))


def masked_scores(query_heads, key_block, positions, score_scale):
    scores = (
        jnp.einsum("nhd,thd->hnt", query_heads, key_block, preferred_element_type=jnp.float32)
        * score_scale
    )
    key_positions = jnp.arange(key_block.shape[0], dtype=jnp.int32)
    visible = key_positions[None, None, :] <= positions[None, :, None]
    return jnp.where(visible, scores, MASKED)


def on_device(
    queries,
    cache_pool,
    lengths,
    block_table,
    out_proj,
    residual_in,
    norm_gain,
    expert_ids,
    route_weight,
    gate_weight,
    up_weight,
    down_weight,
):
    head_dim = cache_pool.shape[3] // 2
    block_len = cache_pool.shape[1]
    max_blocks = cache_pool.shape[0]
    new_rows = queries.shape[0]
    local_heads = queries.shape[1] // head_dim
    score_scale = 1.0 / math.sqrt(head_dim)
    context = lengths[0]
    sequence = cache_pool[block_table[0]]
    kv_choice = (
        lax.axis_index("sec") * local_heads + jnp.arange(local_heads, dtype=jnp.int32)
    ) // (QH // KVH)
    selected = jnp.take(sequence, kv_choice, axis=2)
    key_heads = selected[..., :head_dim]
    value_heads = selected[..., head_dim:]
    query_heads = queries.reshape(new_rows, local_heads, head_dim)
    positions = context - new_rows + jnp.arange(new_rows, dtype=jnp.int32)
    all_keys = key_heads.reshape(max_blocks * block_len, local_heads, head_dim)
    all_values = value_heads.reshape(max_blocks * block_len, local_heads, head_dim)
    scores = masked_scores(query_heads, all_keys, positions, score_scale)
    row_max = jnp.max(scores, axis=-1, keepdims=True)
    exp_scores = jnp.exp(scores - row_max)
    row_sum = jnp.sum(exp_scores, axis=-1, keepdims=True)
    probabilities = (exp_scores / row_sum).astype(jnp.bfloat16)
    attended = jnp.einsum(
        "hnt,thd->nhd", probabilities, all_values, preferred_element_type=jnp.float32
    )
    attn = attended.astype(jnp.bfloat16).reshape(new_rows, local_heads * head_dim)
    share_rows = new_rows // (lax.axis_size("head") * lax.axis_size("sec"))
    partial_value = jnp.dot(attn, out_proj, preferred_element_type=jnp.float32)
    projected = lax.psum_scatter(
        partial_value.astype(jnp.bfloat16).astype(jnp.float32).astype(jnp.bfloat16),
        ("head", "sec"),
        scatter_dimension=0,
        tiled=True,
    ).astype(jnp.float32)
    residual = (residual_in.astype(jnp.float32) + projected).astype(jnp.bfloat16)
    residual_wide = residual.astype(jnp.float32)
    mean_square = jnp.mean(residual_wide * residual_wide, axis=-1, keepdims=True)
    normed = (residual_wide * lax.rsqrt(mean_square + EPSILON) * norm_gain).astype(jnp.bfloat16)
    experts_all = lax.axis_size("head") * lax.axis_size("sec")
    capacity = share_rows * TOP // experts_all
    flat_ids = expert_ids.reshape(-1)
    onehot = (flat_ids[:, None] == jnp.arange(experts_all, dtype=jnp.int32)[None, :]).astype(
        jnp.int32
    )
    before = jnp.cumsum(onehot, axis=0) - onehot
    target = flat_ids * capacity + jnp.sum(before * onehot, axis=1)
    source_row = (
        jnp.zeros((experts_all * capacity,), jnp.int32)
        .at[target]
        .set(jnp.arange(share_rows * TOP, dtype=jnp.int32) // TOP)
    )
    buffer = normed[source_row].reshape(experts_all, capacity, normed.shape[1])
    copies = lax.all_gather(buffer[None], "req", axis=0, tiled=True)
    results = run_expert(
        lax.all_to_all(copies, ("head", "sec"), split_axis=1, concat_axis=1, tiled=True),
        gate_weight,
        up_weight,
        down_weight,
    )
    partial_back = lax.all_to_all(results, ("head", "sec"), split_axis=1, concat_axis=1, tiled=True)
    returned = (
        lax.psum_scatter(
            partial_back.astype(jnp.float32).astype(jnp.bfloat16),
            "req",
            scatter_dimension=0,
            tiled=True,
        )
        .astype(jnp.float32)[0]
        .astype(jnp.bfloat16)
    )
    gathered_out = returned.reshape(experts_all * capacity, -1)[target].reshape(share_rows, TOP, -1)
    expert_mix = jnp.sum(route_weight[:, :, None] * gathered_out.astype(jnp.float32), axis=1)
    return (residual.astype(jnp.float32) + expert_mix).astype(jnp.bfloat16)


def solution(mesh):
    return jax.shard_map(
        on_device,
        mesh=mesh,
        in_specs=(
            P(("groups", "req"), ("head", "sec")),
            P(("groups", "req"), None, "head", None),
            P(("groups", "req")),
            P(("groups", "req"), None),
            P(("head", "sec"), None),
            P(("groups", "req", "head", "sec"), None),
            P(),
            P(("groups", "req", "head", "sec"), None),
            P(("groups", "req", "head", "sec"), None),
            P(("head", "sec"), None, "req"),
            P(("head", "sec"), None, "req"),
            P(("head", "sec"), "req", None),
        ),
        out_specs=P(("groups", "req", "head", "sec"), None),
        check_vma=False,
    )
```

profile of v0, /device:TPU:0, one launch (start us, length us, event | category | flops | bytes accessed | tf_op | source)
XLA Modules:
  0.0 203.9 jit_solution(17053103708731632131)
XLA Ops:
  7.4 4.3 %gather_fusion = bf16[12,128,2,128]{3,2,1,0:T(2,128)(2,1)} fusion(bf16[12,128,2,128]{3,2,1,0:T(2,128)(2,1)} %param.13, s32[1024]{0:T(1024)S(1)} %pad_clamp_fusion.3), kind=kCustom, calls=%fused_computation | custom fusion | bytes 1572912 | tf_op jit(solution)/shard_map/gather | solution.py:58
  11.7 2.2 %copy.61 = bf16[12,128,2,128]{3,1,2,0:T(8,128)(2,1)} copy(bf16[12,128,2,128]{3,2,1,0:T(2,128)(2,1)} %gather_fusion) | data formatting | bytes 1572864 | tf_op jit(solution)/shard_map/gather | solution.py:58
  13.9 3.7 %gather_fusion.1 = bf16[8,12,128,128]{3,2,1,0:T(8,128)(2,1)} fusion(bf16[12,128,2,128]{3,1,2,0:T(8,128)(2,1)} %copy.61, s32[1024]{0:T(1024)S(1)} %pad_clamp_fusion.2), kind=kCustom, calls=%fused_computation.1 | custom fusion | bytes 6291488 | tf_op jit(solution)/shard_map/jit(_take)/gather | solution.py:62
  17.6 2.3 %select_bitcast_fusion = bf16[12,128,8,128]{3,1,0,2:T(8,128)(2,1)S(1)} fusion(bf16[8,12,128,128]{3,2,1,0:T(8,128)(2,1)} %gather_fusion.1, pred[8]{0:T(512)(128)(4,1)S(1)} %compare_and_fusion), kind=kLoop, calls=%fused_computation.18 | loop fusion | flops 1572864 | bytes 6291464 | tf_op jit(solution)/shard_map/jit(_take)/select_n | solution.py:62
  19.9 3.8 %fusion.50 = (bf16[12,128,8,64]{3,1,0,2:T(8,128)(2,1)}, bf16[12,128,8,64]{3,1,0,2:T(8,128)(2,1)}) fusion(bf16[12,128,8,128]{3,1,0,2:T(8,128)(2,1)S(1)} %select_bitcast_fusion), kind=kLoop, calls=%fused_computation.82 | loop fusion | bytes 6291456 | tf_op jit(solution)/shard_map/slice | solution.py:63
  24.7 4.1 %fusion.51 = f32[8,128]{1,0:T(8,128)S(1)} fusion(pred[128,1536]{0,1:T(8,128)(4,1)S(1)} %iota_compare_fusion, bf16[1536,8,64]{2,0,1:T(8,128)(2,1)} %bitcast.70, bf16[128,8,64]{0,2,1:T(8,128)(2,1)S(1)} %bitcast.75), kind=kOutput, calls=%fused_computation.83 | convolution fusion | flops 207619584 | bytes 1904640 | tf_op jit(solution)/shard_map/sub | solution.py:71
  28.7 5.8 %fusion.24 = bf16[8,64,128]{2,1,0:T(8,128)(2,1)S(1)} fusion(bf16[1536,8,64]{2,0,1:T(8,128)(2,1)} %bitcast.72, f32[8,128]{1,0:T(8,128)S(1)} %fusion.51, pred[128,1536]{0,1:T(8,128)(4,1)S(1)} %iota_compare_fusion, bf16[1536,8,64]{2,0,1:T(8,128)(2,1)} %bitcast.71, bf16[128,8,64]{0,2,1:T(8,128)(2,1)S(1)} %bitcast.76), kind=kOutput, calls=%fused_computation.26 | convolution fusion | flops 410585600 | bytes 3608576 | tf_op jit(solution)/shard_map/hnt,thd->nhd/dot_general | solution.py:74
  34.6 2.0 convolution_convert_fusion
  38.2 32.8 %reduce-scatter.3.cloned.1.call-done = bf16[16,2880]{1,0:T(8,128)(2,1)} async-done(((bf16[128,2880]{1,0:T(8,128)(2,1)}), bf16[16,2880]{1,0:T(8,128)(2,1)}) %reduce-scatter.3.cloned.1.call-update) | async-done | bytes 92176 | tf_op jit(solution)/shard_map/reduce_scatter | solution.py:80
  71.0 1.0 fusion.31
  72.0 1.0 fusion.33
  73.8 8.3 %all_gather.3 = bf16[2,8,8,2880]{3,2,1,0:T(8,128)(2,1)S(1)} all-gather(bf16[1,8,8,2880]{3,2,1,0:T(8,128)(2,1)S(1)} %bitcast.74), channel_id=1, replica_groups=mesh['groups'=2,'req'=2,'head'=4,'sec'=2] {'req'}, dimensions={0}, use_global_device_ids=true | all-gather | bytes 1105920 | tf_op jit(solution)/shard_map/all_gather | solution.py:104
  82.2 24.9 %all_to_all.10 = bf16[2,8,8,2880]{3,2,0,1:T(8,128)(2,1)S(1)} all-to-all(bf16[2,8,8,2880]{3,2,0,1:T(8,128)(2,1)S(1)} %copy.69), channel_id=1, replica_groups=mesh['groups'=2,'req'=2,'head'=4,'sec'=2] {'head','sec'}, dimensions={1} | all-to-all | bytes 1474560 | tf_op jit(solution)/shard_map/all_to_all | solution.py:106
  107.1 0.9 copy-done.1
  108.0 6.7 %fusion.5 = f32[128,1440]{0,1:T(8,128)} fusion(bf16[128,2880]{1,0:T(8,128)(2,1)S(1)} %bitcast.68, bf16[1,2880,1440]{1,2,0:T(8,128)(2,1)} %param.21), kind=kOutput, calls=%fused_computation.10 | convolution fusion | flops 1061683200 | bytes 9768960 | tf_op jit(solution)/shard_map/dot_general | solution.py:20
  114.7 15.6 %fusion.8 = bf16[128,2880]{0,1:T(8,128)(2,1)} fusion(bf16[1,1440,2880]{2,1,0:T(8,128)(2,1)} %param.23, bf16[128,2880]{1,0:T(8,128)(2,1)} %bitcast.69, bf16[1,2880,1440]{1,2,0:T(8,128)(2,1)} %param.22, f32[128,1440]{0,1:T(8,128)} %fusion.5), kind=kOutput, calls=%fused_computation.16 | convolution fusion | flops 2125209600 | bytes 18800640 | tf_op jit(solution)/shard_map/dot_general | solution.py:23
  130.3 2.3 %copy.71 = bf16[128,2880]{1,0:T(8,128)(2,1)} copy(bf16[128,2880]{0,1:T(8,128)(2,1)} %fusion.8) | data formatting | bytes 1474560 | tf_op jit(solution)/shard_map/convert_element_type | solution.py:24
  132.6 1.2 copy.72
  133.8 23.4 %all_to_all.11 = bf16[2,8,8,2880]{3,2,0,1:T(8,128)(2,1)} all-to-all(bf16[2,8,8,2880]{3,2,0,1:T(8,128)(2,1)S(1)} %copy.72), channel_id=1, replica_groups=mesh['groups'=2,'req'=2,'head'=4,'sec'=2] {'head','sec'}, dimensions={1} | all-to-all | bytes 1474560 | tf_op jit(solution)/shard_map/all_to_all | solution.py:111
  157.9 31.6 %all-reduce.3.cloned.1.call-done = bf16[2,8,8,2880]{3,2,0,1:T(8,128)(2,1)} async-done(((bf16[2,8,8,2880]{3,2,0,1:T(8,128)(2,1)}), bf16[2,8,8,2880]{3,2,0,1:T(8,128)(2,1)}) %all-reduce.3.cloned.1.call-update) | async-done | bytes 737296
  189.5 1.7 dynamic-slice_bitcast_fusion
  191.2 1.5 gather_fusion.3
  192.7 2.0 %reshape.195 = f32[16,4,2880]{2,1,0:T(4,128)} reshape(bf16[64,2880]{1,0:T(8,128)(2,1)} %gather_fusion.3) | data formatting | bytes 1105920 | tf_op jit(solution)/shard_map/convert_element_type | solution.py:123
  194.7 1.7 multiply_reduce_fusion
  (50 shorter events, 5.0 us)
Async XLA Ops:
  6.5 28.1 %copy-start = (bf16[512,2880]{0,1:T(8,128)(2,1)S(1)}, bf16[512,2880]{0,1:T(8,128)(2,1)}, u32[]{:S(2)}) copy-start(bf16[512,2880]{0,1:T(8,128)(2,1)} %param.16) | copy-start | bytes 8847364
  6.5 64.5 %reduce-scatter.3.cloned.1.call-start = ((), (), s32[]{:S(2)}) async-start(), calls=%async_computation.3 | async-start | bytes 847872 | tf_op jit(solution)/shard_map/reduce_scatter | solution.py:80
  19.9 4.7 %copy-start.4 = (bf16[128,512]{1,0:T(8,128)(2,1)S(1)}, bf16[128,512]{1,0:T(8,128)(2,1)}, u32[]{:S(2)}) copy-start(bf16[128,512]{1,0:T(8,128)(2,1)} %param.12) | copy-start | bytes 393220
  34.6 2.1 %copy-start.6 = (s32[16,4]{0,1:T(4,128)S(1)}, s32[16,4]{0,1:T(4,128)}, u32[]{:S(2)}) copy-start(s32[16,4]{0,1:T(4,128)} %param.19) | copy-start | bytes 772
  34.6 36.4 %copy-start.2 = (bf16[16,2880]{1,0:T(8,128)(2,1)S(1)}, bf16[16,2880]{1,0:T(8,128)(2,1)}, u32[]{:S(2)}) copy-start(bf16[16,2880]{1,0:T(8,128)(2,1)} %param.17) | copy-start | bytes 276484
  34.6 37.5 %copy-start.5 = (f32[2880]{0:T(1024)S(1)}, f32[2880]{0:T(1024)}, u32[]{:S(2)}) copy-start(f32[2880]{0:T(1024)} %param.18) | copy-start | bytes 34564
  36.6 152.9 %all-reduce.3.cloned.1.call-start = ((), (), s32[]{:S(2)}) async-start(), calls=%async_computation.4 | async-start | bytes 1507328
  107.1 0.9 copy-start.1
  130.3 26.9 %copy-start.7 = (f32[16,4]{0,1:T(4,128)S(1)}, f32[16,4]{0,1:T(4,128)}, u32[]{:S(2)}) copy-start(f32[16,4]{0,1:T(4,128)} %param.20) | copy-start | bytes 772
  130.3 27.0 %copy-start.8 = (u32[32]{0:T(128)S(1)}, u32[32]{0:T(128)}, u32[]{:S(2)}) copy-start(u32[32]{0:T(128)} %constant.94) | copy-start | bytes 388
  157.2 39.2 %copy-start.3 = (bf16[16,2880]{1,0:T(8,128)(2,1)S(1)}, bf16[16,2880]{1,0:T(8,128)(2,1)}, u32[]{:S(2)}) copy-start(bf16[16,2880]{1,0:T(8,128)(2,1)} %reduce-scatter.3.cloned.1.call-done) | copy-start | bytes 276484
Sparse Core Ops, SparseCore 0:
  36.7 34.2 reduce-scatter.2
  157.3 32.1 all-reduce.2
where the time goes:
time: 205 us; the launch traced here: 204 us
  waiting for transfers between devices  64.4 us (31%)
  blocking collectives  56.5 us (28%)
  matrix products  34.2 us (17%)
  local copies, waits for them, and re-layouts  26.4 us (13%)
  between operations  14.3 us (7%)
  other arithmetic  7.99 us (4%)
    reduce_scatter x1, waiting for transfers between devices, on_device(): lax.psum_scatter(partial_value.astype(jnp.bfloat16).astype(jnp.float32).a...  32.8 us
    unnamed x3, waiting for transfers between devices  31.7 us
    all_to_all x1, blocking collectives, on_device(): lax.all_to_all(copies, ('head', 'sec'), split_axis=1, concat_axis=1, tile...  24.9 us
    all_to_all x1, blocking collectives, on_device(): lax.all_to_all(results, ('head', 'sec'), split_axis=1, concat_axis=1, til...  23.4 us
    dot_general x1, matrix products, run_expert(): jnp.dot(activated, down_weight[0], preferred_element_type=jnp.float32)  15.6 us
    all_gather x1, blocking collectives, on_device(): copies = lax.all_gather(buffer[None], 'req', axis=0, tiled=True)  8.28 us
    dot_general x1, matrix products, run_expert(): jnp.dot(flat_rows, gate_weight[0], preferred_element_type=jnp.float32)  6.69 us
    gather x2, local copies, waits for them, and re-layouts, on_device(): sequence = cache_pool[block_table[0]]  6.47 us
  transfers between devices with their start and end apart: 2, of which 2 were waited for; matrix products, arithmetic and copies ran while one was open for 1% of the time, Pallas kernels for 0%

commit v1 on v0

--- a/solution.py
+++ b/solution.py
@@ -1,8 +1,11 @@
+import functools
 import math
 
 import jax
 import jax.numpy as jnp
 from jax import lax
+from jax.experimental import pallas as pl
+from jax.experimental.pallas import tpu as pltpu
 from jax.sharding import PartitionSpec as P
 
 QH = 64
@@ -12,6 +15,7 @@
 
 EPSILON = 1e-05
 MASKED = -1e30
+CHUNK = 768
 
 
 def run_expert(row_block, gate_weight, up_weight, down_weight):
@@ -124,9 +128,383 @@
     return (residual.astype(jnp.float32) + expert_mix).astype(jnp.bfloat16)
 
 
+def lane_chunks(width, size):
+    return [(start, min(size, width - start)) for start in range(0, width, size)]
+
+
+def layer_kernel(
+    chunks,
+    meta_col,
+    experts,
+    q_ref,
+    kv_ref,
+    len_ref,
+    bt_ref,
+    wo_ref,
+    res_ref,
+    gain_ref,
+    ids_ref,
+    rw_ref,
+    wg_hbm,
+    wu_hbm,
+    wd_hbm,
+    out_ref,
+    wg,
+    wu,
+    wd,
+    attn,
+    psend,
+    precv,
+    pown,
+    zsend,
+    zrecv,
+    resid,
+    xbuf,
+    xs,
+    act,
+    w_sem,
+    core_send,
+    core_recv,
+    x_send,
+    x_recv,
+    z_send,
+    z_recv,
+    *chunk_refs,
+):
+    g, r = lax.axis_index("groups"), lax.axis_index("req")
+    h, s = lax.axis_index("head"), lax.axis_index("sec")
+    heads = attn.shape[0]
+    share = attn.shape[2]
+    depth = res_ref.shape[1]
+    f32, bf16 = jnp.float32, jnp.bfloat16
+
+    weight_copies = [
+        pltpu.make_async_copy(src.at[0], dst, w_sem.at[i])
+        for i, (src, dst) in enumerate(((wg_hbm, wg), (wu_hbm, wu), (wd_hbm, wd)))
+    ]
+    for copy in weight_copies:
+        copy.start()
+
+    core_dev = (g, r, h, 1 - s)
+    x_dev = (g, 1 - r, h, s)
+    z_devs = [(g, r, lax.rem(h + j, heads), s) for j in range(1, heads)]
+    barrier = pltpu.get_barrier_semaphore()
+    for device in [core_dev, x_dev] + z_devs:
+        pl.semaphore_signal(
+            barrier, inc=1, device_id=device, device_id_type=pl.DeviceIdType.MESH
+        )
+
+    def remote(src, dst, send_sem, recv_sem, device):
+        return pltpu.make_async_remote_copy(
+            src_ref=src,
+            dst_ref=dst,
+            send_sem=send_sem,
+            recv_sem=recv_sem,
+            device_id=device,
+            device_id_type=pl.DeviceIdType.MESH,
+        )
+
+    tokens = kv_ref.shape[0]
+    new_rows = q_ref.shape[0]
+    blocks = bt_ref.shape[1]
+    block_len = tokens // blocks
+    lane_t = lax.broadcasted_iota(jnp.int32, (1, tokens), 1)
+    stored = lane_t // block_len
+    place = jnp.zeros((1, tokens), jnp.int32)
+    for i in range(blocks):
+        place = jnp.where(stored == bt_ref[0, i], i, place)
+    key_pos = place * block_len + lane_t % block_len - (len_ref[0] - new_rows)
+    row_pos = lax.broadcasted_iota(jnp.int32, (2 * new_rows, 1), 0) % new_rows
+    visible = key_pos <= row_pos
+    lane_q = lax.broadcasted_iota(jnp.int32, (new_rows, 128), 1)
+    low = lane_q < 64
+    for pair in range(q_ref.shape[1] // 128):
+        both = q_ref[:, pair * 128 : (pair + 1) * 128].astype(f32) * 0.125
+        even = jnp.where(low, both, 0.0)
+        odd = jnp.where(low, pltpu.roll(both, 64, axis=1), 0.0)
+        stacked = jnp.concatenate([even, odd], axis=0).astype(bf16)
+        scores = lax.dot_general(
+            stacked, kv_ref[...], (((1,), (1,)), ((), ())), preferred_element_type=f32
+        )
+        scores = jnp.where(visible, scores, MASKED)
+        top = jnp.max(scores, axis=-1, keepdims=True)
+        weights = jnp.exp(scores - top)
+        total = jnp.sum(weights, axis=-1, keepdims=True)
+        mixed = jnp.dot(weights.astype(bf16), kv_ref[...], preferred_element_type=f32) / total
+        joined = jnp.where(low, pltpu.roll(mixed[:new_rows], 64, axis=1), mixed[new_rows:])
+        attn[:, :, :, pair * 128 : (pair + 1) * 128] = joined.astype(bf16).reshape(
+            heads, 2, share, 128
+        )
+
+    inner = attn.shape[3]
+    psend[...] = jnp.dot(
+        attn[:, 1 - s].reshape(heads * share, inner), wo_ref[...], preferred_element_type=f32
+    ).astype(bf16)
+    pl.semaphore_wait(barrier, 1 + heads)
+    pair_copy = remote(psend, precv, core_send.at[0], core_recv.at[0], core_dev)
+    pair_copy.start()
+    pown[...] = jnp.dot(
+        attn[:, s].reshape(heads * share, inner), wo_ref[...], preferred_element_type=f32
+    ).reshape(heads, share, depth)
+    pair_copy.wait_recv()
+    pown[...] = pown[...] + precv[...].reshape(heads, share, depth).astype(f32)
+    zsend[...] = pown[...].astype(bf16)
+    order = sorted(range(1, heads), key=lambda j: -min(j, heads - j))
+    z_copies = {}
+    for j in order:
+        z_copies[j] = remote(
+            zsend.at[lax.rem(h + j, heads)],
+            zrecv.at[j - 1],
+            z_send.at[j - 1],
+            z_recv.at[j - 1],
+            z_devs[j - 1],
+        )
+        z_copies[j].start()
+    sent = [pair_copy] + list(z_copies.values())
+
+    lane_e = lax.broadcasted_iota(jnp.int32, (share, 128), 1)
+    dense = jnp.zeros((share, 128), f32)
+    for k in range(ids_ref.shape[1]):
+        chosen = ids_ref[:, k : k + 1]
+        dense = dense + jnp.where(
+            (lane_e == chosen) | (lane_e == chosen + experts), rw_ref[:, k : k + 1], 0.0
+        )
+    coarse = dense.astype(bf16).astype(f32)
+    meta = jnp.where(lane_e < experts, coarse, dense - coarse).astype(bf16)
+
+    gathered = res_ref[...].astype(f32) + pown[h]
+    for j in range(1, heads):
+        z_copies[j].wait_recv()
+        gathered = gathered + zrecv[j - 1].astype(f32)
+    residual = gathered.astype(bf16)
+    resid[...] = residual
+    wide = residual.astype(f32)
+    mean_square = jnp.mean(wide * wide, axis=-1, keepdims=True)
+    normed = (wide * lax.rsqrt(mean_square + EPSILON) * gain_ref[...]).astype(bf16)
+    xbuf[r, h, s, :, :depth] = normed
+    xbuf[r, h, s, :, meta_col:] = meta
+
+    def spread(rr, j, send_sem, recv_sem, device):
+        block = xbuf.at[rr, lax.rem(h - j + heads, heads), s]
+        return remote(block, block, send_sem, recv_sem, device)
+
+    zg = {
+        j: spread(r, 0, z_send.at[2 + j], z_recv.at[2 + j], z_devs[j - 1])
+        for j in range(1, heads)
+    }
+    xg = {j: spread(r, j, x_send.at[j], x_recv.at[j], x_dev) for j in range(heads)}
+    cg = {
+        j: spread(r, j, core_send.at[1 + j], core_recv.at[1 + j], core_dev) for j in range(heads)
+    }
+    cx = {
+        j: spread(
+            1 - r, j, core_send.at[1 + heads + j], core_recv.at[1 + heads + j], core_dev
+        )
+        for j in range(heads)
+    }
+    for j in order:
+        zg[j].start()
+    xg[0].start()
+    cg[0].start()
+    near_first = order[::-1]
+    for j in near_first:
+        zg[j].wait_recv()
+        xg[j].start()
+        cg[j].start()
+    for j in [0] + near_first:
+        xg[j].wait_recv()
+        cx[j].start()
+    for j in range(heads):
+        cg[j].wait_recv()
+    for j in range(heads):
+        cx[j].wait_recv()
+    sent += list(zg.values()) + list(xg.values()) + list(cg.values()) + list(cx.values())
+
+    half = 2 * heads * share
+    xs[:half] = xbuf[:, :, 1 - s, :, :depth].reshape(half, depth)
+    xs[half:] = xbuf[:, :, s, :, :depth].reshape(half, depth)
+    expert = h * 2 + s
+    lane_w = lax.broadcasted_iota(jnp.int32, (half, 128), 1)
+    mine = (lane_w == expert) | (lane_w == expert + experts)
+
+    def route_column(core):
+        packed = xbuf[:, :, core, :, meta_col:].reshape(half, 128).astype(f32)
+        return jnp.sum(jnp.where(mine, packed, 0.0), axis=-1, keepdims=True)
+
+    other_weight = route_column(1 - s)
+    own_weight = route_column(s)
+    weight_copies[0].wait()
+    weight_copies[1].wait()
+
+    def hidden_tile(tile):
+        gate_out = jnp.dot(xs[...], wg[:, tile], preferred_element_type=f32)
+        up_out = jnp.dot(xs[...], wu[:, tile], preferred_element_type=f32)
+        act[:, tile] = (gate_out * jax.nn.sigmoid(1.702 * gate_out) * (up_out + 1.0)).astype(bf16)
+
+    hidden = wg.shape[1]
+    full = hidden // 256
+
+    @pl.loop(0, full)
+    def _(i):
+        hidden_tile(pl.ds(pl.multiple_of(i * 256, 256), 256))
+
+    if hidden % 256:
+        hidden_tile(pl.ds(full * 256, hidden % 256))
+    weight_copies[2].wait()
+
+    count = len(chunks)
+    per = len(chunk_refs) // count
+    base_core, base_x, base_z = 1 + 2 * heads, heads, 2 * (heads - 1)
+    core_copies, x_copies, line_copies = {}, {}, {}
+
+    def multiply(c):
+        csend, crecv, cown, xsend, xrecv, zsend2, zrecv2 = chunk_refs[c * per : (c + 1) * per]
+        start, width = chunks[c]
+        product = jnp.dot(act[...], wd[:, start : start + width], preferred_element_type=f32)
+        csend[...] = (product[:half] * other_weight).astype(bf16).reshape(2, heads, share, width)
+        core_copies[c] = remote(
+            csend, crecv, core_send.at[base_core + c], core_recv.at[base_core + c], core_dev
+        )
+        core_copies[c].start()
+        cown[...] = (product[half:] * own_weight).reshape(2, heads, share, width)
+
+    def over_core(c):
+        csend, crecv, cown, xsend, xrecv, zsend2, zrecv2 = chunk_refs[c * per : (c + 1) * per]
+        core_copies[c].wait_recv()
+        xsend[...] = (cown[1 - r] + crecv[1 - r].astype(f32)).astype(bf16)
+        x_copies[c] = remote(xsend, xrecv, x_send.at[base_x + c], x_recv.at[base_x + c], x_dev)
+        x_copies[c].start()
+        cown[r] = cown[r] + crecv[r].astype(f32)
+
+    def over_req(c):
+        csend, crecv, cown, xsend, xrecv, zsend2, zrecv2 = chunk_refs[c * per : (c + 1) * per]
+        x_copies[c].wait_recv()
+        cown[r] = cown[r] + xrecv[...].astype(f32)
+        zsend2[...] = cown[r].astype(bf16)
+        line_copies[c] = {}
+        for j in order:
+            sem = base_z + c * (heads - 1) + j - 1
+            line_copies[c][j] = remote(
+                zsend2.at[lax.rem(h + j, heads)],
+                zrecv2.at[j - 1],
+                z_send.at[sem],
+                z_recv.at[sem],
+                z_devs[j - 1],
+            )
+            line_copies[c][j].start()
+
+    def over_line(c):
+        csend, crecv, cown, xsend, xrecv, zsend2, zrecv2 = chunk_refs[c * per : (c + 1) * per]
+        start, width = chunks[c]
+        total = resid[:, start : start + width].astype(f32) + cown[r, h]
+        for j in range(1, heads):
+            line_copies[c][j].wait_recv()
+            total = total + zrecv2[j - 1].astype(f32)
+        out_ref[:, start : start + width] = total.astype(bf16)
+
+    for step in range(count + 3):
+        for lag, stage in enumerate((multiply, over_core, over_req, over_line)):
+            if 0 <= step - lag < count:
+                stage(step - lag)
+    sent += list(core_copies.values()) + list(x_copies.values())
+    for copies in line_copies.values():
+        sent += list(copies.values())
+    for copy in sent:
+        copy.wait_send()
+
+
+def fused_on_device(
+    queries,
+    cache_pool,
+    lengths,
+    block_table,
+    out_proj,
+    residual_in,
+    norm_gain,
+    expert_ids,
+    route_weight,
+    gate_weight,
+    up_weight,
+    down_weight,
+):
+    bf16, f32 = jnp.bfloat16, jnp.float32
+    heads = lax.axis_size("head")
+    share, depth = residual_in.shape
+    inner = queries.shape[1]
+    hidden = gate_weight.shape[2]
+    experts = heads * 2
+    tokens = cache_pool.shape[0] * cache_pool.shape[1]
+    kv = lax.dynamic_index_in_dim(cache_pool, lax.axis_index("sec"), axis=2, keepdims=False)
+    kv = kv.reshape(tokens, cache_pool.shape[3])
+    meta_col = -(-depth // 128) * 128
+    chunks = lane_chunks(depth, CHUNK)
+    count = len(chunks)
+    vmem = pltpu.VMEM
+    scratch = [
+        vmem((depth, hidden), bf16),
+        vmem((depth, hidden), bf16),
+        vmem((hidden, depth), bf16),
+        vmem((heads, 2, share, inner), bf16),
+        vmem((heads * share, depth), bf16),
+        vmem((heads * share, depth), bf16),
+        vmem((heads, share, depth), f32),
+        vmem((heads, share, depth), bf16),
+        vmem((heads - 1, share, depth), bf16),
+        vmem((share, depth), bf16),
+        vmem((2, heads, 2, share, meta_col + 128), bf16),
+        vmem((4 * heads * share, depth), bf16),
+        vmem((4 * heads * share, hidden), bf16),
+        pltpu.SemaphoreType.DMA((3,)),
+        pltpu.SemaphoreType.DMA((1 + 2 * heads + count,)),
+        pltpu.SemaphoreType.DMA((1 + 2 * heads + count,)),
+        pltpu.SemaphoreType.DMA((heads + count,)),
+        pltpu.SemaphoreType.DMA((heads + count,)),
+        pltpu.SemaphoreType.DMA(((heads - 1) * (2 + count),)),
+        pltpu.SemaphoreType.DMA(((heads - 1) * (2 + count),)),
+    ]
+    for start, width in chunks:
+        scratch += [
+            vmem((2, heads, share, width), bf16),
+            vmem((2, heads, share, width), bf16),
+            vmem((2, heads, share, width), f32),
+            vmem((heads, share, width), bf16),
+            vmem((heads, share, width), bf16),
+            vmem((heads, share, width), bf16),
+            vmem((heads - 1, share, width), bf16),
+        ]
+    in_vmem = pl.BlockSpec(memory_space=pltpu.VMEM)
+    in_smem = pl.BlockSpec(memory_space=pltpu.SMEM)
+    in_place = pl.BlockSpec(memory_space=pl.ANY)
+    return pl.pallas_call(
+        functools.partial(layer_kernel, chunks, meta_col, experts),
+        out_shape=jax.ShapeDtypeStruct((share, depth), bf16),
+        in_specs=[in_vmem, in_vmem, in_smem, in_smem] + [in_vmem] * 5 + [in_place] * 3,
+        out_specs=in_vmem,
+        scratch_shapes=scratch,
+        compiler_params=pltpu.CompilerParams(
+            collective_id=0, has_side_effects=True, vmem_limit_bytes=58 << 20
+        ),
+    )(
+        queries,
+        kv,
+        lengths,
+        block_table,
+        out_proj,
+        residual_in,
+        norm_gain[None, :],
+        expert_ids,
+        route_weight,
+        gate_weight,
+        up_weight,
+        down_weight,
+    )
+
+
 def solution(mesh):
+    sizes = dict(mesh.shape)
+    fused = sizes["req"] == 2 and sizes["sec"] == 2 and sizes["head"] == 4
     return jax.shard_map(
-        on_device,
+        fused_on_device if fused else on_device,
         mesh=mesh,
         in_specs=(
             P(("groups", "req"), ("head", "sec")),

time: 205 us -> 102 us (0.50)
  Pallas kernels: 0 us -> 64.8 us
  waiting for transfers between devices: 64.4 us -> 0 us
  blocking collectives: 56.5 us -> 0 us
  matrix products: 34.2 us -> 0 us
  between operations: 14.3 us -> 0.75 us
  local copies, waits for them, and re-layouts: 26.4 us -> 35.2 us
  other arithmetic: 7.99 us -> 0 us
    pallas_call x0 -> x1, Pallas kernels: none -> 64.8 us  [fused_on_device(): pl.pallas_call(functools.partial(layer_kernel, chunks, meta_col, experts)...]
    all_to_all x2 -> x0, blocking collectives: 48.3 us -> none  [the longest x1 24.9 us: on_device(): lax.all_to_all(copies, ('head', 'sec'), split_axis=1, concat_axis=1, tile...]
    reduce_scatter x1 -> x0, waiting for transfers between devices: 32.8 us -> none  [on_device(): lax.psum_scatter(partial_value.astype(jnp.bfloat16).astype(jnp.float32).a...]
    unnamed x3 -> x0, waiting for transfers between devices: 31.7 us -> none
    unnamed x22 -> x9, local copies, waits for them, and re-layouts: 1.77 us -> 32.9 us
    dot_general x4 -> x0, matrix products: 30.1 us -> none  [the longest x1 15.6 us: run_expert(): jnp.dot(activated, down_weight[0], preferred_element_type=jnp.float32)]
    gather x5 -> x0, local copies, waits for them, and re-layouts: 12.5 us -> none  [the longest x2 6.47 us: on_device(): sequence = cache_pool[block_table[0]]]
    all_gather x1 -> x0, blocking collectives: 8.28 us -> none  [on_device(): copies = lax.all_gather(buffer[None], 'req', axis=0, tiled=True)]
  transfers between devices with their start and end apart: 2 -> 0, of which waited for: 2 -> 0; matrix products, arithmetic and copies ran while one was open for 1% -> 0% of each run, Pallas kernels for 0% -> 0%
where the time goes in v1:
time: 102 us; the launch traced here: 101 us
  Pallas kernels  64.8 us (64%)
  local copies, waits for them, and re-layouts  35.2 us (35%)
    pallas_call x1, Pallas kernels, fused_on_device(): pl.pallas_call(functools.partial(layer_kernel, chunks, meta_col, experts)...  64.8 us
    unnamed x9, local copies, waits for them, and re-layouts  32.9 us

profile of v1, /device:TPU:0, one launch (start us, length us, event | category | flops | bytes accessed | tf_op | source)
XLA Modules:
  0.0 100.7 jit_solution(4263132240096157253)
XLA Ops:
  0.0 0.0 copy-start
  0.7 1.4 %copy.20.ids_ref = s32[16,4]{1,0:T(8,128)} copy(s32[16,4]{0,1:T(4,128)} %param.19) | data formatting | bytes 512 | tf_op args[7]
  2.1 1.4 %copy.21.rw_ref = f32[16,4]{1,0:T(8,128)} copy(f32[16,4]{0,1:T(4,128)} %param.20) | data formatting | bytes 512 | tf_op args[8]
  3.4 1.3 %broadcast_in_dim.3.gain_ref = f32[1,2880]{1,0:T(1,128)} reshape(f32[2880]{0:T(1024)} %param.18) | data formatting | bytes 23040 | tf_op jit(solution)/shard_map/broadcast_in_dim | solution.py:494
  4.8 0.0 copy-done
  4.8 0.9 constant_dynamic-slice_fusion
  5.7 0.8 copy.24
  6.5 4.6 %copy.19.wo_ref = bf16[512,2880]{1,0:T(8,128)(2,1)} copy(bf16[512,2880]{0,1:T(8,128)(2,1)} %param.16) | data formatting | bytes 5898240 | tf_op args[4]
  11.1 11.6 %copy.22.wg_hbm = bf16[1,2880,1440]{2,1,0:T(8,128)(2,1)} copy(bf16[1,2880,1440]{1,2,0:T(8,128)(2,1)} %param.21) | data formatting | bytes 16588800 | tf_op args[9]
  22.7 11.7 %copy.23.wu_hbm = bf16[1,2880,1440]{2,1,0:T(8,128)(2,1)} copy(bf16[1,2880,1440]{1,2,0:T(8,128)(2,1)} %param.22) | data formatting | bytes 16588800 | tf_op args[10]
  34.4 64.8 %shard_map.118 = bf16[16,2880]{1,0:T(8,128)(2,1)} custom-call(bf16[128,512]{1,0:T(8,128)(2,1)} %q_ref.1, bf16[1536,128]{1,0:T(8,128)(2,1)} %bitcast.1, s32[1]{0:T(128)S(6)} %copy.26.len_ref, s32[1,12]{1,0:T(1,128)} %bt_ref.1, bf16[512,2880]{1,0:T(8,128)(2,1)} %copy.19.wo_ref, bf16[16,2880]{1,0:T(8,128)(2,1)} %res_ref.1, f32[1,2880]{1,0:T(1,128)} %broadcast_in_dim.3.gain_ref, ...), custom_call_target="tpu_custom_call" | custom-call | tf_op jit(solution)/shard_map/pallas_call | solution.py:478
  99.1 1.5 %copy.27 = bf16[16,2880]{1,0:T(8,128)(2,1)} copy(bf16[16,2880]{1,0:T(8,128)(2,1)} %shard_map.118) | data formatting | bytes 184320
Async XLA Ops:
  0.0 4.8 %copy-start = (bf16[12,128,2,128]{3,2,1,0:T(2,128)(2,1)S(1)}, bf16[12,128,2,128]{3,2,1,0:T(2,128)(2,1)}, u32[]{:S(2)}) copy-start(bf16[12,128,2,128]{3,2,1,0:T(2,128)(2,1)} %param.13) | copy-start | bytes 2359300

commit v2 on v1

--- a/solution.py
+++ b/solution.py
@@ -130,6 +130,12 @@
 
 def lane_chunks(width, size):
     return [(start, min(size, width - start)) for start in range(0, width, size)]
+
+
+def dot_rows(rows, weight_rows):
+    return lax.dot_general(
+        rows, weight_rows, (((1,), (1,)), ((), ())), preferred_element_type=jnp.float32
+    )
 
 
 def layer_kernel(
@@ -223,9 +229,7 @@
         even = jnp.where(low, both, 0.0)
         odd = jnp.where(low, pltpu.roll(both, 64, axis=1), 0.0)
         stacked = jnp.concatenate([even, odd], axis=0).astype(bf16)
-        scores = lax.dot_general(
-            stacked, kv_ref[...], (((1,), (1,)), ((), ())), preferred_element_type=f32
-        )
+        scores = dot_rows(stacked, kv_ref[...])
         scores = jnp.where(visible, scores, MASKED)
         top = jnp.max(scores, axis=-1, keepdims=True)
         weights = jnp.exp(scores - top)
@@ -237,15 +241,13 @@
         )
 
     inner = attn.shape[3]
-    psend[...] = jnp.dot(
-        attn[:, 1 - s].reshape(heads * share, inner), wo_ref[...], preferred_element_type=f32
-    ).astype(bf16)
+    psend[...] = dot_rows(attn[:, 1 - s].reshape(heads * share, inner), wo_ref[...]).astype(bf16)
     pl.semaphore_wait(barrier, 1 + heads)
     pair_copy = remote(psend, precv, core_send.at[0], core_recv.at[0], core_dev)
     pair_copy.start()
-    pown[...] = jnp.dot(
-        attn[:, s].reshape(heads * share, inner), wo_ref[...], preferred_element_type=f32
-    ).reshape(heads, share, depth)
+    pown[...] = dot_rows(attn[:, s].reshape(heads * share, inner), wo_ref[...]).reshape(
+        heads, share, depth
+    )
     pair_copy.wait_recv()
     pown[...] = pown[...] + precv[...].reshape(heads, share, depth).astype(f32)
     zsend[...] = pown[...].astype(bf16)
@@ -263,12 +265,14 @@
     sent = [pair_copy] + list(z_copies.values())
 
     lane_e = lax.broadcasted_iota(jnp.int32, (share, 128), 1)
-    dense = jnp.zeros((share, 128), f32)
-    for k in range(ids_ref.shape[1]):
-        chosen = ids_ref[:, k : k + 1]
-        dense = dense + jnp.where(
-            (lane_e == chosen) | (lane_e == chosen + experts), rw_ref[:, k : k + 1], 0.0
-        )
+    line_e = lax.broadcasted_iota(jnp.int32, (128, share), 0)
+    by_expert = jnp.zeros((128, share), f32)
+    for k in range(ids_ref.shape[0]):
+        chosen = ids_ref[k : k + 1, :]
+        by_expert = by_expert + jnp.where(
+            (line_e == chosen) | (line_e == chosen + experts), rw_ref[k : k + 1, :], 0.0
+        )
+    dense = by_expert.T
     coarse = dense.astype(bf16).astype(f32)
     meta = jnp.where(lane_e < experts, coarse, dense - coarse).astype(bf16)
 
@@ -280,7 +284,7 @@
     resid[...] = residual
     wide = residual.astype(f32)
     mean_square = jnp.mean(wide * wide, axis=-1, keepdims=True)
-    normed = (wide * lax.rsqrt(mean_square + EPSILON) * gain_ref[...]).astype(bf16)
+    normed = (wide * lax.rsqrt(mean_square + EPSILON) * gain_ref[...][None, :]).astype(bf16)
     xbuf[r, h, s, :, :depth] = normed
     xbuf[r, h, s, :, meta_col:] = meta
 
@@ -337,11 +341,11 @@
     weight_copies[1].wait()
 
     def hidden_tile(tile):
-        gate_out = jnp.dot(xs[...], wg[:, tile], preferred_element_type=f32)
-        up_out = jnp.dot(xs[...], wu[:, tile], preferred_element_type=f32)
+        gate_out = dot_rows(xs[...], wg[tile, :])
+        up_out = dot_rows(xs[...], wu[tile, :])
         act[:, tile] = (gate_out * jax.nn.sigmoid(1.702 * gate_out) * (up_out + 1.0)).astype(bf16)
 
-    hidden = wg.shape[1]
+    hidden = wg.shape[0]
     full = hidden // 256
 
     @pl.loop(0, full)
@@ -441,8 +445,8 @@
     count = len(chunks)
     vmem = pltpu.VMEM
     scratch = [
-        vmem((depth, hidden), bf16),
-        vmem((depth, hidden), bf16),
+        vmem((hidden, depth), bf16),
+        vmem((hidden, depth), bf16),
         vmem((hidden, depth), bf16),
         vmem((heads, 2, share, inner), bf16),
         vmem((heads * share, depth), bf16),
@@ -489,13 +493,13 @@
         kv,
         lengths,
         block_table,
-        out_proj,
+        out_proj.T,
         residual_in,
-        norm_gain[None, :],
-        expert_ids,
-        route_weight,
-        gate_weight,
-        up_weight,
+        norm_gain,
+        expert_ids.T,
+        route_weight.T,
+        jnp.swapaxes(gate_weight, 1, 2),
+        jnp.swapaxes(up_weight, 1, 2),
         down_weight,
     )
 

time: 102 us -> 70.6 us (0.69); the launches traced: 101 us -> 70.4 us
  local copies, waits for them, and re-layouts: 35.2 us -> 4.42 us
    unnamed x9 -> x4, local copies, waits for them, and re-layouts: 32.9 us -> 3.48 us
    broadcast_in_dim x1 -> x0, local copies, waits for them, and re-layouts: 1.31 us -> none  [fused_on_device(): norm_gain[None, :]]
where the time goes in v2:
time: 70.6 us; the launch traced here: 70.4 us
  Pallas kernels  65.3 us (92%)
  local copies, waits for them, and re-layouts  4.42 us (6%)
    pallas_call x1, Pallas kernels, fused_on_device(): pl.pallas_call(functools.partial(layer_kernel, chunks, meta_col, experts)...  65.3 us
    unnamed x4, local copies, waits for them, and re-layouts  3.48 us

profile of v2, /device:TPU:0, one launch (start us, length us, event | category | flops | bytes accessed | tf_op | source)
XLA Modules:
  0.0 70.4 jit_solution(7738266609061669714)
XLA Ops:
  0.0 0.0 copy-start
  0.0 1.1 %copy-done = bf16[12,128,2,128]{3,2,1,0:T(2,128)(2,1)S(1)} copy-done((bf16[12,128,2,128]{3,2,1,0:T(2,128)(2,1)S(1)}, bf16[12,128,2,128]{3,2,1,0:T(2,128)(2,1)}, u32[]{:S(2)}) %copy-start) | copy-done | bytes 786456
  1.1 0.9 %constant_dynamic-slice_fusion = bf16[12,128,1,128]{3,2,1,0:T(2,128)(2,1)S(1)} fusion(bf16[12,128,2,128]{3,2,1,0:T(2,128)(2,1)S(1)} %copy-done, s32[]{:T(128)S(6)} %select_n.4), kind=kLoop, calls=%fused_computation | loop fusion | bytes 786436 | tf_op jit(solution)/shard_map/jit(dynamic_index_in_dim)/dynamic_slice | solution.py:441
  2.1 0.8 %copy.14 = bf16[12,128,1,128]{3,1,0,2:T(8,128)(2,1)} copy(bf16[12,128,1,128]{3,2,1,0:T(2,128)(2,1)S(1)} %constant_dynamic-slice_fusion) | data formatting | bytes 786432
  3.5 65.3 %shard_map.118 = bf16[16,2880]{1,0:T(8,128)(2,1)} custom-call(bf16[128,512]{1,0:T(8,128)(2,1)} %q_ref.1, bf16[1536,128]{1,0:T(8,128)(2,1)} %bitcast.9, s32[1]{0:T(128)S(6)} %copy.16.len_ref, s32[1,12]{1,0:T(1,128)} %bt_ref.1, bf16[2880,512]{1,0:T(8,128)(2,1)} %bitcast.8, bf16[16,2880]{1,0:T(8,128)(2,1)} %res_ref.1, f32[2880]{0:T(1024)} %gain_ref.1, ...), custom_call_target="tpu_custom_call" | custom-call | tf_op jit(solution)/shard_map/pallas_call | solution.py:482
  68.8 1.5 %copy.17 = bf16[16,2880]{1,0:T(8,128)(2,1)} copy(bf16[16,2880]{1,0:T(8,128)(2,1)} %shard_map.118) | data formatting | bytes 184320
Async XLA Ops:
  0.0 1.1 %copy-start = (bf16[12,128,2,128]{3,2,1,0:T(2,128)(2,1)S(1)}, bf16[12,128,2,128]{3,2,1,0:T(2,128)(2,1)}, u32[]{:S(2)}) copy-start(bf16[12,128,2,128]{3,2,1,0:T(2,128)(2,1)} %param.13) | copy-start | bytes 2359300

commit v3 on v2

--- a/solution.py
+++ b/solution.py
@@ -140,8 +140,6 @@
 
 def layer_kernel(
     chunks,
-    meta_col,
-    experts,
     q_ref,
     kv_ref,
     len_ref,
@@ -165,8 +163,8 @@
     zsend,
     zrecv,
     resid,
-    xbuf,
-    xs,
+    disp,
+    xin,
     act,
     w_sem,
     core_send,
@@ -182,6 +180,7 @@
     heads = attn.shape[0]
     share = attn.shape[2]
     depth = res_ref.shape[1]
+    cap = disp.shape[2]
     f32, bf16 = jnp.float32, jnp.bfloat16
 
     weight_copies = [
@@ -195,7 +194,8 @@
     x_dev = (g, 1 - r, h, s)
     z_devs = [(g, r, lax.rem(h + j, heads), s) for j in range(1, heads)]
     barrier = pltpu.get_barrier_semaphore()
-    for device in [core_dev, x_dev] + z_devs:
+    far_devs = [(g, r, lax.rem(h + j, heads), 1 - s) for j in range(1, heads)]
+    for device in [core_dev, x_dev] + z_devs + far_devs:
         pl.semaphore_signal(
             barrier, inc=1, device_id=device, device_id_type=pl.DeviceIdType.MESH
         )
@@ -242,7 +242,7 @@
 
     inner = attn.shape[3]
     psend[...] = dot_rows(attn[:, 1 - s].reshape(heads * share, inner), wo_ref[...]).astype(bf16)
-    pl.semaphore_wait(barrier, 1 + heads)
+    pl.semaphore_wait(barrier, 2 * heads)
     pair_copy = remote(psend, precv, core_send.at[0], core_recv.at[0], core_dev)
     pair_copy.start()
     pown[...] = dot_rows(attn[:, s].reshape(heads * share, inner), wo_ref[...]).reshape(
@@ -264,17 +264,25 @@
         z_copies[j].start()
     sent = [pair_copy] + list(z_copies.values())
 
-    lane_e = lax.broadcasted_iota(jnp.int32, (share, 128), 1)
-    line_e = lax.broadcasted_iota(jnp.int32, (128, share), 0)
-    by_expert = jnp.zeros((128, share), f32)
+    slots = 2 * heads * cap
+    slot = lax.broadcasted_iota(jnp.int32, (slots, share), 0)
+    named = jnp.zeros((slots, share), f32)
+    routed = jnp.zeros((slots, share), f32)
     for k in range(ids_ref.shape[0]):
-        chosen = ids_ref[k : k + 1, :]
-        by_expert = by_expert + jnp.where(
-            (line_e == chosen) | (line_e == chosen + experts), rw_ref[k : k + 1, :], 0.0
-        )
-    dense = by_expert.T
-    coarse = dense.astype(bf16).astype(f32)
-    meta = jnp.where(lane_e < experts, coarse, dense - coarse).astype(bf16)
+        hit = ids_ref[k : k + 1, :] == slot // cap
+        named = named + jnp.where(hit, 1.0, 0.0)
+        routed = routed + jnp.where(hit, rw_ref[k : k + 1, :], 0.0)
+    earlier = lax.broadcasted_iota(jnp.int32, (share, share), 0) < lax.broadcasted_iota(
+        jnp.int32, (share, share), 1
+    )
+    rank = jnp.dot(
+        named.astype(bf16), jnp.where(earlier, 1.0, 0.0).astype(bf16), preferred_element_type=f32
+    )
+    rank_here = jnp.where(rank == (slot % cap).astype(f32), 1.0, 0.0)
+    pick = (named * rank_here).astype(bf16)
+    mix = (routed * rank_here).T
+    mix_coarse = mix.astype(bf16)
+    mix_fine = (mix - mix_coarse.astype(f32)).astype(bf16)
 
     gathered = res_ref[...].astype(f32) + pown[h]
     for j in range(1, heads):
@@ -285,64 +293,53 @@
     wide = residual.astype(f32)
     mean_square = jnp.mean(wide * wide, axis=-1, keepdims=True)
     normed = (wide * lax.rsqrt(mean_square + EPSILON) * gain_ref[...][None, :]).astype(bf16)
-    xbuf[r, h, s, :, :depth] = normed
-    xbuf[r, h, s, :, meta_col:] = meta
-
-    def spread(rr, j, send_sem, recv_sem, device):
-        block = xbuf.at[rr, lax.rem(h - j + heads, heads), s]
-        return remote(block, block, send_sem, recv_sem, device)
-
-    zg = {
-        j: spread(r, 0, z_send.at[2 + j], z_recv.at[2 + j], z_devs[j - 1])
-        for j in range(1, heads)
-    }
-    xg = {j: spread(r, j, x_send.at[j], x_recv.at[j], x_dev) for j in range(heads)}
-    cg = {
-        j: spread(r, j, core_send.at[1 + j], core_recv.at[1 + j], core_dev) for j in range(heads)
-    }
-    cx = {
-        j: spread(
-            1 - r, j, core_send.at[1 + heads + j], core_recv.at[1 + heads + j], core_dev
+    disp[...] = (
+        jnp.dot(pick, normed, preferred_element_type=f32)
+        .astype(bf16)
+        .reshape(heads, 2, cap, depth)
+    )
+    xin[r, h, s] = disp[h, s]
+
+    def peer(j, other):
+        return lax.rem(h + j, heads), (1 - s if other else s)
+
+    def source(j, other):
+        return lax.rem(h - j + heads, heads), (1 - s if other else s)
+
+    near_first = order[::-1]
+    routes = [(0, 1)] + [(j, other) for j in near_first for other in (0, 1)]
+    routed_copies = {}
+    for j, other in routes:
+        to_h, to_s = peer(j, other)
+        sem = heads - 1 + 2 * j + other
+        routed_copies[j, other] = remote(
+            disp.at[to_h, to_s],
+            xin.at[r, h, s],
+            z_send.at[sem],
+            z_recv.at[sem],
+            (g, r, to_h, to_s),
         )
-        for j in range(heads)
-    }
-    for j in order:
-        zg[j].start()
-    xg[0].start()
-    cg[0].start()
-    near_first = order[::-1]
-    for j in near_first:
-        zg[j].wait_recv()
-        xg[j].start()
-        cg[j].start()
-    for j in [0] + near_first:
-        xg[j].wait_recv()
-        cx[j].start()
-    for j in range(heads):
-        cg[j].wait_recv()
-    for j in range(heads):
-        cx[j].wait_recv()
-    sent += list(zg.values()) + list(xg.values()) + list(cg.values()) + list(cx.values())
-
-    half = 2 * heads * share
-    xs[:half] = xbuf[:, :, 1 - s, :, :depth].reshape(half, depth)
-    xs[half:] = xbuf[:, :, s, :, :depth].reshape(half, depth)
-    expert = h * 2 + s
-    lane_w = lax.broadcasted_iota(jnp.int32, (half, 128), 1)
-    mine = (lane_w == expert) | (lane_w == expert + experts)
-
-    def route_column(core):
-        packed = xbuf[:, :, core, :, meta_col:].reshape(half, 128).astype(f32)
-        return jnp.sum(jnp.where(mine, packed, 0.0), axis=-1, keepdims=True)
-
-    other_weight = route_column(1 - s)
-    own_weight = route_column(s)
+        routed_copies[j, other].start()
+    across = {}
+    for j, other in [(0, 0)] + routes:
+        if (j, other) != (0, 0):
+            routed_copies[j, other].wait_recv()
+        from_h, from_s = source(j, other)
+        block = xin.at[r, from_h, from_s]
+        sem = 2 * j + other
+        across[j, other] = remote(block, block, x_send.at[sem], x_recv.at[sem], x_dev)
+        across[j, other].start()
+    for copy in across.values():
+        copy.wait_recv()
+    sent += list(routed_copies.values()) + list(across.values())
+
+    rows_in = 4 * heads * cap
     weight_copies[0].wait()
     weight_copies[1].wait()
 
     def hidden_tile(tile):
-        gate_out = dot_rows(xs[...], wg[tile, :])
-        up_out = dot_rows(xs[...], wu[tile, :])
+        gate_out = dot_rows(xin[...].reshape(rows_in, depth), wg[tile, :])
+        up_out = dot_rows(xin[...].reshape(rows_in, depth), wu[tile, :])
         act[:, tile] = (gate_out * jax.nn.sigmoid(1.702 * gate_out) * (up_out + 1.0)).astype(bf16)
 
     hidden = wg.shape[0]
@@ -358,59 +355,54 @@
 
     count = len(chunks)
     per = len(chunk_refs) // count
-    base_core, base_x, base_z = 1 + 2 * heads, heads, 2 * (heads - 1)
-    core_copies, x_copies, line_copies = {}, {}, {}
+    base_x, base_z = 2 * heads, 3 * heads - 1
+    x_copies, line_copies = {}, {}
+    back = [(j, other) for j in order for other in (0, 1)] + [(0, 1)]
 
     def multiply(c):
-        csend, crecv, cown, xsend, xrecv, zsend2, zrecv2 = chunk_refs[c * per : (c + 1) * per]
+        cown, xsend, xrecv, back_send, back_recv = chunk_refs[c * per : (c + 1) * per]
         start, width = chunks[c]
-        product = jnp.dot(act[...], wd[:, start : start + width], preferred_element_type=f32)
-        csend[...] = (product[:half] * other_weight).astype(bf16).reshape(2, heads, share, width)
-        core_copies[c] = remote(
-            csend, crecv, core_send.at[base_core + c], core_recv.at[base_core + c], core_dev
-        )
-        core_copies[c].start()
-        cown[...] = (product[half:] * own_weight).reshape(2, heads, share, width)
-
-    def over_core(c):
-        csend, crecv, cown, xsend, xrecv, zsend2, zrecv2 = chunk_refs[c * per : (c + 1) * per]
-        core_copies[c].wait_recv()
-        xsend[...] = (cown[1 - r] + crecv[1 - r].astype(f32)).astype(bf16)
+        cown[...] = jnp.dot(
+            act[...], wd[:, start : start + width], preferred_element_type=f32
+        ).reshape(2, heads, 2, cap, width)
+        xsend[...] = cown[1 - r].astype(bf16)
         x_copies[c] = remote(xsend, xrecv, x_send.at[base_x + c], x_recv.at[base_x + c], x_dev)
         x_copies[c].start()
-        cown[r] = cown[r] + crecv[r].astype(f32)
 
     def over_req(c):
-        csend, crecv, cown, xsend, xrecv, zsend2, zrecv2 = chunk_refs[c * per : (c + 1) * per]
+        cown, xsend, xrecv, back_send, back_recv = chunk_refs[c * per : (c + 1) * per]
         x_copies[c].wait_recv()
-        cown[r] = cown[r] + xrecv[...].astype(f32)
-        zsend2[...] = cown[r].astype(bf16)
+        back_send[...] = (cown[r].astype(bf16).astype(f32) + xrecv[...].astype(f32)).astype(bf16)
         line_copies[c] = {}
-        for j in order:
-            sem = base_z + c * (heads - 1) + j - 1
-            line_copies[c][j] = remote(
-                zsend2.at[lax.rem(h + j, heads)],
-                zrecv2.at[j - 1],
+        for j, other in back:
+            to_h, to_s = peer(j, other)
+            sem = base_z + c * 2 * heads + 2 * j + other
+            line_copies[c][j, other] = remote(
+                back_send.at[to_h, to_s],
+                back_recv.at[h, s],
                 z_send.at[sem],
                 z_recv.at[sem],
-                z_devs[j - 1],
+                (g, r, to_h, to_s),
             )
-            line_copies[c][j].start()
-
-    def over_line(c):
-        csend, crecv, cown, xsend, xrecv, zsend2, zrecv2 = chunk_refs[c * per : (c + 1) * per]
+            line_copies[c][j, other].start()
+        back_recv[h, s] = back_send[h, s]
+
+    def at_rows(c):
+        cown, xsend, xrecv, back_send, back_recv = chunk_refs[c * per : (c + 1) * per]
         start, width = chunks[c]
-        total = resid[:, start : start + width].astype(f32) + cown[r, h]
-        for j in range(1, heads):
-            line_copies[c][j].wait_recv()
-            total = total + zrecv2[j - 1].astype(f32)
+        for copy in line_copies[c].values():
+            copy.wait_recv()
+        outs = back_recv[...].reshape(slots, width)
+        total = jnp.dot(mix_coarse, outs, preferred_element_type=f32)
+        total = total + jnp.dot(mix_fine, outs, preferred_element_type=f32)
+        total = total + resid[:, start : start + width].astype(f32)
         out_ref[:, start : start + width] = total.astype(bf16)
 
-    for step in range(count + 3):
-        for lag, stage in enumerate((multiply, over_core, over_req, over_line)):
+    for step in range(count + 2):
+        for lag, stage in enumerate((multiply, over_req, at_rows)):
             if 0 <= step - lag < count:
                 stage(step - lag)
-    sent += list(core_copies.values()) + list(x_copies.values())
+    sent += list(x_copies.values())
     for copies in line_copies.values():
         sent += list(copies.values())
     for copy in sent:
@@ -436,11 +428,10 @@
     share, depth = residual_in.shape
     inner = queries.shape[1]
     hidden = gate_weight.shape[2]
-    experts = heads * 2
+    cap = share * TOP // (heads * 2)
     tokens = cache_pool.shape[0] * cache_pool.shape[1]
     kv = lax.dynamic_index_in_dim(cache_pool, lax.axis_index("sec"), axis=2, keepdims=False)
     kv = kv.reshape(tokens, cache_pool.shape[3])
-    meta_col = -(-depth // 128) * 128
     chunks = lane_chunks(depth, CHUNK)
     count = len(chunks)
     vmem = pltpu.VMEM
@@ -455,32 +446,30 @@
         vmem((heads, share, depth), bf16),
         vmem((heads - 1, share, depth), bf16),
         vmem((share, depth), bf16),
-        vmem((2, heads, 2, share, meta_col + 128), bf16),
-        vmem((4 * heads * share, depth), bf16),
-        vmem((4 * heads * share, hidden), bf16),
+        vmem((heads, 2, cap, depth), bf16),
+        vmem((2, heads, 2, cap, depth), bf16),
+        vmem((4 * heads * cap, hidden), bf16),
         pltpu.SemaphoreType.DMA((3,)),
-        pltpu.SemaphoreType.DMA((1 + 2 * heads + count,)),
-        pltpu.SemaphoreType.DMA((1 + 2 * heads + count,)),
-        pltpu.SemaphoreType.DMA((heads + count,)),
-        pltpu.SemaphoreType.DMA((heads + count,)),
-        pltpu.SemaphoreType.DMA(((heads - 1) * (2 + count),)),
-        pltpu.SemaphoreType.DMA(((heads - 1) * (2 + count),)),
+        pltpu.SemaphoreType.DMA((1,)),
+        pltpu.SemaphoreType.DMA((1,)),
+        pltpu.SemaphoreType.DMA((2 * heads + count,)),
+        pltpu.SemaphoreType.DMA((2 * heads + count,)),
+        pltpu.SemaphoreType.DMA((heads - 1 + 2 * heads * (1 + count),)),
+        pltpu.SemaphoreType.DMA((heads - 1 + 2 * heads * (1 + count),)),
     ]
     for start, width in chunks:
         scratch += [
-            vmem((2, heads, share, width), bf16),
-            vmem((2, heads, share, width), bf16),
-            vmem((2, heads, share, width), f32),
-            vmem((heads, share, width), bf16),
-            vmem((heads, share, width), bf16),
-            vmem((heads, share, width), bf16),
-            vmem((heads - 1, share, width), bf16),
+            vmem((2, heads, 2, cap, width), f32),
+            vmem((heads, 2, cap, width), bf16),
+            vmem((heads, 2, cap, width), bf16),
+            vmem((heads, 2, cap, width), bf16),
+            vmem((heads, 2, cap, width), bf16),
         ]
     in_vmem = pl.BlockSpec(memory_space=pltpu.VMEM)
     in_smem = pl.BlockSpec(memory_space=pltpu.SMEM)
     in_place = pl.BlockSpec(memory_space=pl.ANY)
     return pl.pallas_call(
-        functools.partial(layer_kernel, chunks, meta_col, experts),
+        functools.partial(layer_kernel, chunks),
         out_shape=jax.ShapeDtypeStruct((share, depth), bf16),
         in_specs=[in_vmem, in_vmem, in_smem, in_smem] + [in_vmem] * 5 + [in_place] * 3,
         out_specs=in_vmem,

time: 70.6 us -> 66.4 us (0.941)
  Pallas kernels: 65.3 us -> 61.1 us
    pallas_call x1, Pallas kernels: 65.3 us -> 61.1 us  [fused_on_device(): pl.pallas_call(functools.partial(layer_kernel, chunks), out_shape=jax.Sha...]
where the time goes in v3:
time: 66.4 us; the launch traced here: 66.2 us
  Pallas kernels  61.1 us (92%)
  local copies, waits for them, and re-layouts  4.42 us (7%)
  between operations  0.67 us (1%)
    pallas_call x1, Pallas kernels, fused_on_device(): pl.pallas_call(functools.partial(layer_kernel, chunks), out_shape=jax.Sha...  61.1 us
    unnamed x4, local copies, waits for them, and re-layouts  3.48 us

profile of v3, /device:TPU:0, one launch (start us, length us, event | category | flops | bytes accessed | tf_op | source)
XLA Modules:
  0.0 66.2 jit_solution(6874067363993976524)
XLA Ops:
  0.0 0.0 copy-start
  0.0 1.1 %copy-done = bf16[12,128,2,128]{3,2,1,0:T(2,128)(2,1)S(1)} copy-done((bf16[12,128,2,128]{3,2,1,0:T(2,128)(2,1)S(1)}, bf16[12,128,2,128]{3,2,1,0:T(2,128)(2,1)}, u32[]{:S(2)}) %copy-start) | copy-done | bytes 786456
  1.1 0.9 %constant_dynamic-slice_fusion = bf16[12,128,1,128]{3,2,1,0:T(2,128)(2,1)S(1)} fusion(bf16[12,128,2,128]{3,2,1,0:T(2,128)(2,1)S(1)} %copy-done, s32[]{:T(128)S(6)} %select_n.4), kind=kLoop, calls=%fused_computation | loop fusion | bytes 786436 | tf_op jit(solution)/shard_map/jit(dynamic_index_in_dim)/dynamic_slice | solution.py:433
  2.1 0.8 %copy.14 = bf16[12,128,1,128]{3,1,0,2:T(8,128)(2,1)} copy(bf16[12,128,1,128]{3,2,1,0:T(2,128)(2,1)S(1)} %constant_dynamic-slice_fusion) | data formatting | bytes 786432
  3.5 61.1 %shard_map.118 = bf16[16,2880]{1,0:T(8,128)(2,1)} custom-call(bf16[128,512]{1,0:T(8,128)(2,1)} %q_ref.1, bf16[1536,128]{1,0:T(8,128)(2,1)} %bitcast.9, s32[1]{0:T(128)S(6)} %copy.16.len_ref, s32[1,12]{1,0:T(1,128)} %bt_ref.1, bf16[2880,512]{1,0:T(8,128)(2,1)} %bitcast.8, bf16[16,2880]{1,0:T(8,128)(2,1)} %res_ref.1, f32[2880]{0:T(1024)} %gain_ref.1, ...), custom_call_target="tpu_custom_call" | custom-call | tf_op jit(solution)/shard_map/pallas_call | solution.py:471
  64.6 1.5 %copy.17 = bf16[16,2880]{1,0:T(8,128)(2,1)} copy(bf16[16,2880]{1,0:T(8,128)(2,1)} %shard_map.118) | data formatting | bytes 184320
Async XLA Ops:
  0.0 1.1 %copy-start = (bf16[12,128,2,128]{3,2,1,0:T(2,128)(2,1)S(1)}, bf16[12,128,2,128]{3,2,1,0:T(2,128)(2,1)}, u32[]{:S(2)}) copy-start(bf16[12,128,2,128]{3,2,1,0:T(2,128)(2,1)} %param.13) | copy-start | bytes 2359300

commit v4 on v3

--- a/solution.py
+++ b/solution.py
@@ -164,6 +164,7 @@
     zrecv,
     resid,
     disp,
+    zin,
     xin,
     act,
     w_sem,
@@ -194,8 +195,7 @@
     x_dev = (g, 1 - r, h, s)
     z_devs = [(g, r, lax.rem(h + j, heads), s) for j in range(1, heads)]
     barrier = pltpu.get_barrier_semaphore()
-    far_devs = [(g, r, lax.rem(h + j, heads), 1 - s) for j in range(1, heads)]
-    for device in [core_dev, x_dev] + z_devs + far_devs:
+    for device in [core_dev, x_dev] + z_devs:
         pl.semaphore_signal(
             barrier, inc=1, device_id=device, device_id_type=pl.DeviceIdType.MESH
         )
@@ -242,7 +242,7 @@
 
     inner = attn.shape[3]
     psend[...] = dot_rows(attn[:, 1 - s].reshape(heads * share, inner), wo_ref[...]).astype(bf16)
-    pl.semaphore_wait(barrier, 2 * heads)
+    pl.semaphore_wait(barrier, 1 + heads)
     pair_copy = remote(psend, precv, core_send.at[0], core_recv.at[0], core_dev)
     pair_copy.start()
     pown[...] = dot_rows(attn[:, s].reshape(heads * share, inner), wo_ref[...]).reshape(
@@ -298,40 +298,46 @@
         .astype(bf16)
         .reshape(heads, 2, cap, depth)
     )
-    xin[r, h, s] = disp[h, s]
-
-    def peer(j, other):
-        return lax.rem(h + j, heads), (1 - s if other else s)
-
-    def source(j, other):
-        return lax.rem(h - j + heads, heads), (1 - s if other else s)
+    zin[h] = disp[h]
 
     near_first = order[::-1]
-    routes = [(0, 1)] + [(j, other) for j in near_first for other in (0, 1)]
-    routed_copies = {}
-    for j, other in routes:
-        to_h, to_s = peer(j, other)
-        sem = heads - 1 + 2 * j + other
-        routed_copies[j, other] = remote(
-            disp.at[to_h, to_s],
-            xin.at[r, h, s],
+    line_in, to_core, across = {}, {}, {}
+    for j in near_first:
+        sem = heads - 2 + j
+        line_in[j] = remote(
+            disp.at[lax.rem(h + j, heads)],
+            zin.at[h],
             z_send.at[sem],
             z_recv.at[sem],
-            (g, r, to_h, to_s),
-        )
-        routed_copies[j, other].start()
-    across = {}
-    for j, other in [(0, 0)] + routes:
-        if (j, other) != (0, 0):
-            routed_copies[j, other].wait_recv()
-        from_h, from_s = source(j, other)
-        block = xin.at[r, from_h, from_s]
-        sem = 2 * j + other
-        across[j, other] = remote(block, block, x_send.at[sem], x_recv.at[sem], x_dev)
-        across[j, other].start()
+            z_devs[j - 1],
+        )
+        line_in[j].start()
+
+    def cross(j, core):
+        block = xin.at[r, lax.rem(h - j + heads, heads), core]
+        sem = 2 * j + (0 if core is s else 1)
+        across[sem] = remote(block, block, x_send.at[sem], x_recv.at[sem], x_dev)
+        across[sem].start()
+
+    for j in [0] + near_first:
+        if j:
+            line_in[j].wait_recv()
+        origin = lax.rem(h - j + heads, heads)
+        to_core[j] = remote(
+            zin.at[origin, 1 - s],
+            xin.at[r, origin, s],
+            core_send.at[1 + j],
+            core_recv.at[1 + j],
+            core_dev,
+        )
+        to_core[j].start()
+        xin[r, origin, s] = zin[origin, s]
+        cross(j, s)
+        to_core[j].wait_recv()
+        cross(j, 1 - s)
     for copy in across.values():
         copy.wait_recv()
-    sent += list(routed_copies.values()) + list(across.values())
+    sent += list(line_in.values()) + list(to_core.values()) + list(across.values())
 
     rows_in = 4 * heads * cap
     weight_copies[0].wait()
@@ -355,12 +361,11 @@
 
     count = len(chunks)
     per = len(chunk_refs) // count
-    base_x, base_z = 2 * heads, 3 * heads - 1
-    x_copies, line_copies = {}, {}
-    back = [(j, other) for j in order for other in (0, 1)] + [(0, 1)]
+    base_core, base_x, base_z = 1 + heads, 2 * heads, 2 * (heads - 1)
+    x_copies, core_copies, line_copies = {}, {}, {}
 
     def multiply(c):
-        cown, xsend, xrecv, back_send, back_recv = chunk_refs[c * per : (c + 1) * per]
+        cown, xsend, xrecv, to_other, back_send, back_recv = chunk_refs[c * per : (c + 1) * per]
         start, width = chunks[c]
         cown[...] = jnp.dot(
             act[...], wd[:, start : start + width], preferred_element_type=f32
@@ -370,25 +375,37 @@
         x_copies[c].start()
 
     def over_req(c):
-        cown, xsend, xrecv, back_send, back_recv = chunk_refs[c * per : (c + 1) * per]
+        cown, xsend, xrecv, to_other, back_send, back_recv = chunk_refs[c * per : (c + 1) * per]
         x_copies[c].wait_recv()
-        back_send[...] = (cown[r].astype(bf16).astype(f32) + xrecv[...].astype(f32)).astype(bf16)
+        to_other[...] = (cown[r].astype(bf16).astype(f32) + xrecv[...].astype(f32)).astype(bf16)
+        core_copies[c] = remote(
+            to_other.at[:, 1 - s],
+            back_send.at[:, s],
+            core_send.at[base_core + c],
+            core_recv.at[base_core + c],
+            core_dev,
+        )
+        core_copies[c].start()
+        back_send[:, s] = to_other[:, s]
+
+    def along_line(c):
+        cown, xsend, xrecv, to_other, back_send, back_recv = chunk_refs[c * per : (c + 1) * per]
+        core_copies[c].wait_recv()
         line_copies[c] = {}
-        for j, other in back:
-            to_h, to_s = peer(j, other)
-            sem = base_z + c * 2 * heads + 2 * j + other
-            line_copies[c][j, other] = remote(
-                back_send.at[to_h, to_s],
-                back_recv.at[h, s],
+        for j in order:
+            sem = base_z + c * (heads - 1) + j - 1
+            line_copies[c][j] = remote(
+                back_send.at[lax.rem(h + j, heads)],
+                back_recv.at[h],
                 z_send.at[sem],
                 z_recv.at[sem],
-                (g, r, to_h, to_s),
+                z_devs[j - 1],
             )
-            line_copies[c][j, other].start()
-        back_recv[h, s] = back_send[h, s]
+            line_copies[c][j].start()
+        back_recv[h] = back_send[h]
 
     def at_rows(c):
-        cown, xsend, xrecv, back_send, back_recv = chunk_refs[c * per : (c + 1) * per]
+        cown, xsend, xrecv, to_other, back_send, back_recv = chunk_refs[c * per : (c + 1) * per]
         start, width = chunks[c]
         for copy in line_copies[c].values():
             copy.wait_recv()
@@ -398,11 +415,15 @@
         total = total + resid[:, start : start + width].astype(f32)
         out_ref[:, start : start + width] = total.astype(bf16)
 
-    for step in range(count + 2):
-        for lag, stage in enumerate((multiply, over_req, at_rows)):
+    for c in range(count):
+        multiply(c)
+    for step in range(count + 1):
+        for lag, stage in enumerate((over_req, along_line)):
             if 0 <= step - lag < count:
                 stage(step - lag)
-    sent += list(x_copies.values())
+    for c in range(count):
+        at_rows(c)
+    sent += list(x_copies.values()) + list(core_copies.values())
     for copies in line_copies.values():
         sent += list(copies.values())
     for copy in sent:
@@ -447,19 +468,21 @@
         vmem((heads - 1, share, depth), bf16),
         vmem((share, depth), bf16),
         vmem((heads, 2, cap, depth), bf16),
+        vmem((heads, 2, cap, depth), bf16),
         vmem((2, heads, 2, cap, depth), bf16),
         vmem((4 * heads * cap, hidden), bf16),
         pltpu.SemaphoreType.DMA((3,)),
-        pltpu.SemaphoreType.DMA((1,)),
-        pltpu.SemaphoreType.DMA((1,)),
+        pltpu.SemaphoreType.DMA((1 + heads + count,)),
+        pltpu.SemaphoreType.DMA((1 + heads + count,)),
         pltpu.SemaphoreType.DMA((2 * heads + count,)),
         pltpu.SemaphoreType.DMA((2 * heads + count,)),
-        pltpu.SemaphoreType.DMA((heads - 1 + 2 * heads * (1 + count),)),
-        pltpu.SemaphoreType.DMA((heads - 1 + 2 * heads * (1 + count),)),
+        pltpu.SemaphoreType.DMA(((heads - 1) * (2 + count),)),
+        pltpu.SemaphoreType.DMA(((heads - 1) * (2 + count),)),
     ]
     for start, width in chunks:
         scratch += [
             vmem((2, heads, 2, cap, width), f32),
+            vmem((heads, 2, cap, width), bf16),
             vmem((heads, 2, cap, width), bf16),
             vmem((heads, 2, cap, width), bf16),
             vmem((heads, 2, cap, width), bf16),

time: 66.4 us -> 64.4 us (0.970)
  Pallas kernels: 61.1 us -> 59.1 us
    pallas_call x1, Pallas kernels: 61.1 us -> 59.1 us  [fused_on_device(): pl.pallas_call(functools.partial(layer_kernel, chunks), out_shape=jax.Sha...]
where the time goes in v4:
time: 64.4 us; the launch traced here: 64.2 us
  Pallas kernels  59.1 us (92%)
  local copies, waits for them, and re-layouts  4.42 us (7%)
  between operations  0.67 us (1%)
    pallas_call x1, Pallas kernels, fused_on_device(): pl.pallas_call(functools.partial(layer_kernel, chunks), out_shape=jax.Sha...  59.1 us
    unnamed x4, local copies, waits for them, and re-layouts  3.48 us

profile of v4, /device:TPU:0, one launch (start us, length us, event | category | flops | bytes accessed | tf_op | source)
XLA Modules:
  0.0 64.2 jit_solution(11849231893828251824)
XLA Ops:
  0.0 0.0 copy-start
  0.0 1.1 %copy-done = bf16[12,128,2,128]{3,2,1,0:T(2,128)(2,1)S(1)} copy-done((bf16[12,128,2,128]{3,2,1,0:T(2,128)(2,1)S(1)}, bf16[12,128,2,128]{3,2,1,0:T(2,128)(2,1)}, u32[]{:S(2)}) %copy-start) | copy-done | bytes 786456
  1.1 0.9 %constant_dynamic-slice_fusion = bf16[12,128,1,128]{3,2,1,0:T(2,128)(2,1)S(1)} fusion(bf16[12,128,2,128]{3,2,1,0:T(2,128)(2,1)S(1)} %copy-done, s32[]{:T(128)S(6)} %select_n.4), kind=kLoop, calls=%fused_computation | loop fusion | bytes 786436 | tf_op jit(solution)/shard_map/jit(dynamic_index_in_dim)/dynamic_slice | solution.py:454
  2.1 0.8 %copy.14 = bf16[12,128,1,128]{3,1,0,2:T(8,128)(2,1)} copy(bf16[12,128,1,128]{3,2,1,0:T(2,128)(2,1)S(1)} %constant_dynamic-slice_fusion) | data formatting | bytes 786432
  3.5 59.1 %shard_map.118 = bf16[16,2880]{1,0:T(8,128)(2,1)} custom-call(bf16[128,512]{1,0:T(8,128)(2,1)} %q_ref.1, bf16[1536,128]{1,0:T(8,128)(2,1)} %bitcast.9, s32[1]{0:T(128)S(6)} %copy.16.len_ref, s32[1,12]{1,0:T(1,128)} %bt_ref.1, bf16[2880,512]{1,0:T(8,128)(2,1)} %bitcast.8, bf16[16,2880]{1,0:T(8,128)(2,1)} %res_ref.1, f32[2880]{0:T(1024)} %gain_ref.1, ...), custom_call_target="tpu_custom_call" | custom-call | tf_op jit(solution)/shard_map/pallas_call | solution.py:494
  62.7 1.5 %copy.17 = bf16[16,2880]{1,0:T(8,128)(2,1)} copy(bf16[16,2880]{1,0:T(8,128)(2,1)} %shard_map.118) | data formatting | bytes 184320
Async XLA Ops:
  0.0 1.1 %copy-start = (bf16[12,128,2,128]{3,2,1,0:T(2,128)(2,1)S(1)}, bf16[12,128,2,128]{3,2,1,0:T(2,128)(2,1)}, u32[]{:S(2)}) copy-start(bf16[12,128,2,128]{3,2,1,0:T(2,128)(2,1)} %param.13) | copy-start | bytes 2359300

commit v5 on v4

--- a/solution.py
+++ b/solution.py
@@ -15,7 +15,7 @@
 
 EPSILON = 1e-05
 MASKED = -1e30
-CHUNK = 768
+CHUNK = 512
 
 
 def run_expert(row_block, gate_weight, up_weight, down_weight):
@@ -349,14 +349,14 @@
         act[:, tile] = (gate_out * jax.nn.sigmoid(1.702 * gate_out) * (up_out + 1.0)).astype(bf16)
 
     hidden = wg.shape[0]
-    full = hidden // 256
+    full = hidden // 512
 
     @pl.loop(0, full)
     def _(i):
-        hidden_tile(pl.ds(pl.multiple_of(i * 256, 256), 256))
-
-    if hidden % 256:
-        hidden_tile(pl.ds(full * 256, hidden % 256))
+        hidden_tile(pl.ds(pl.multiple_of(i * 512, 512), 512))
+
+    if hidden % 512:
+        hidden_tile(pl.ds(full * 512, hidden % 512))
     weight_copies[2].wait()
 
     count = len(chunks)

time: 64.4 us -> 63.2 us (0.981)
  Pallas kernels: 59.1 us -> 57.9 us
    pallas_call x1, Pallas kernels: 59.1 us -> 57.9 us  [fused_on_device(): pl.pallas_call(functools.partial(layer_kernel, chunks), out_shape=jax.Sha...]
where the time goes in v5:
time: 63.2 us; the launch traced here: 63 us
  Pallas kernels  57.9 us (92%)
  local copies, waits for them, and re-layouts  4.42 us (7%)
  between operations  0.67 us (1%)
    pallas_call x1, Pallas kernels, fused_on_device(): pl.pallas_call(functools.partial(layer_kernel, chunks), out_shape=jax.Sha...  57.9 us
    unnamed x4, local copies, waits for them, and re-layouts  3.48 us

profile of v5, /device:TPU:0, one launch (start us, length us, event | category | flops | bytes accessed | tf_op | source)
XLA Modules:
  0.0 63.0 jit_solution(15453761385885733307)
XLA Ops:
  0.0 0.0 copy-start
  0.0 1.1 %copy-done = bf16[12,128,2,128]{3,2,1,0:T(2,128)(2,1)S(1)} copy-done((bf16[12,128,2,128]{3,2,1,0:T(2,128)(2,1)S(1)}, bf16[12,128,2,128]{3,2,1,0:T(2,128)(2,1)}, u32[]{:S(2)}) %copy-start) | copy-done | bytes 786456
  1.1 0.9 %constant_dynamic-slice_fusion = bf16[12,128,1,128]{3,2,1,0:T(2,128)(2,1)S(1)} fusion(bf16[12,128,2,128]{3,2,1,0:T(2,128)(2,1)S(1)} %copy-done, s32[]{:T(128)S(6)} %select_n.4), kind=kLoop, calls=%fused_computation | loop fusion | bytes 786436 | tf_op jit(solution)/shard_map/jit(dynamic_index_in_dim)/dynamic_slice | solution.py:454
  2.1 0.8 %copy.14 = bf16[12,128,1,128]{3,1,0,2:T(8,128)(2,1)} copy(bf16[12,128,1,128]{3,2,1,0:T(2,128)(2,1)S(1)} %constant_dynamic-slice_fusion) | data formatting | bytes 786432
  3.5 57.9 %shard_map.118 = bf16[16,2880]{1,0:T(8,128)(2,1)} custom-call(bf16[128,512]{1,0:T(8,128)(2,1)} %q_ref.1, bf16[1536,128]{1,0:T(8,128)(2,1)} %bitcast.9, s32[1]{0:T(128)S(6)} %copy.16.len_ref, s32[1,12]{1,0:T(1,128)} %bt_ref.1, bf16[2880,512]{1,0:T(8,128)(2,1)} %bitcast.8, bf16[16,2880]{1,0:T(8,128)(2,1)} %res_ref.1, f32[2880]{0:T(1024)} %gain_ref.1, ...), custom_call_target="tpu_custom_call" | custom-call | tf_op jit(solution)/shard_map/pallas_call | solution.py:494
  61.4 1.5 %copy.17 = bf16[16,2880]{1,0:T(8,128)(2,1)} copy(bf16[16,2880]{1,0:T(8,128)(2,1)} %shard_map.118) | data formatting | bytes 184320
Async XLA Ops:
  0.0 1.1 %copy-start = (bf16[12,128,2,128]{3,2,1,0:T(2,128)(2,1)S(1)}, bf16[12,128,2,128]{3,2,1,0:T(2,128)(2,1)}, u32[]{:S(2)}) copy-start(bf16[12,128,2,128]{3,2,1,0:T(2,128)(2,1)} %param.13) | copy-start | bytes 2359300
